TPU v7x, 32 devices: a whole 2x2x4 slice. The times are simulated.
32 devices in a mesh: rep: 4 (over y, x), fsdp: 8 (over z, core).
Axes of the slice: x: 2, y: 2, z: 4, core: 2. Of those that a mesh axis runs over, the one named last changes fastest.
Arguments:
- params: bfloat16 [2, 8192, 4608], P(None, 'fsdp'), may hold values from -6 to 6
- deltas: bfloat16 [4, 2, 8192, 4608], P('rep', None, 'fsdp'), may hold values from -3 to 3
- momentum: float32 [2, 8192, 4608], P(None, 'fsdp', 'rep'), may hold values from -2 to 2
Outputs:
- new_params: bfloat16 [2, 8192, 4608], P(None, 'fsdp')
- new_momentum: float32 [2, 8192, 4608], P(None, 'fsdp', 'rep')
All inputs are finite; a program needn't handle non-finite values.
Results may differ from a plain program's by a relative error of at most 0.0035.
Values may be sent and summed in bfloat16 or wider, within the bound.
A program may use at most 192 MiB of HBM per device.

v0:
```python
import jax
import jax.numpy as jnp
from jax import lax
from jax.sharding import PartitionSpec as P

Q_ROWS = 4096
KV_ROWS = 2048


clip_share = 0.5
peak_eps = 1e-06
outer_rate = 0.7
momentum_decay = 0.9


def apply_update(summed, tau_rows, param_piece, moment, replicas):
    outer = tau_rows[..., None] * summed / jnp.float32(replicas)
    fresh_moment = momentum_decay * moment + outer
    fresh = (
        param_piece.astype(jnp.float32) - outer_rate * (outer + momentum_decay * fresh_moment)
    ).astype(jnp.bfloat16)
    return (fresh, fresh_moment)


def on_device(params, deltas, momentum):
    local = deltas[0]
    shard_rows = local.shape[1]
    row_ids = lax.axis_index("fsdp") * shard_rows + lax.iota(jnp.int32, shard_rows)
    tensor_ids = (row_ids >= Q_ROWS).astype(jnp.int32) + (row_ids >= Q_ROWS + KV_ROWS).astype(
        jnp.int32
    )
    member = tensor_ids[None, :] == lax.iota(jnp.int32, 3)[:, None]
    row_peak = jnp.max(jnp.abs(local), axis=2).astype(jnp.float32)
    local_peak = jnp.max(jnp.where(member[None], row_peak[:, None, :], jnp.float32(0.0)), axis=2)
    peak = lax.pmax(local_peak, ("rep", "fsdp"))
    scaled = clip_share * (peak + peak_eps)
    tau = jnp.sum(jnp.where(member[None], scaled[:, :, None], jnp.float32(0.0)), axis=1)
    codes = jnp.clip(local.astype(jnp.float32) / tau[..., None], -1.0, 1.0).astype(jnp.bfloat16)
    replicas = lax.axis_size("rep")
    owned = momentum.shape[2]
    start = lax.axis_index("rep") * owned
    param_piece = lax.dynamic_slice_in_dim(params, start, owned, 2)
    gathered_layers = []
    moment_layers = []
    for layer in range(codes.shape[0]):
        summed = lax.psum_scatter(codes[layer], "rep", scatter_dimension=1, tiled=True).astype(
            jnp.float32
        )
        fresh, fresh_moment = apply_update(
            summed, tau[layer], param_piece[layer], momentum[layer], replicas
        )
        gathered_layers.append(lax.all_gather(fresh, "rep", axis=1, tiled=True))
        moment_layers.append(fresh_moment)
    new_params = jnp.stack(gathered_layers, axis=0)
    new_momentum = jnp.stack(moment_layers, axis=0)
    return (new_params, new_momentum)


def solution(mesh):
    placed = (P(None, "fsdp", None), P("rep", None, "fsdp", None), P(None, "fsdp", "rep"))
    return jax.shard_map(
        on_device,
        mesh=mesh,
        in_specs=placed,
        out_specs=(P(None, "fsdp", None), P(None, "fsdp", "rep")),
        check_vma=False,
    )
```

profile of v0, /device:TPU:0, one launch (start us, length us, event | category | flops | bytes accessed | tf_op | source)
XLA Modules:
  0.0 514.7 jit_solution(11386809934413209248)
XLA Ops:
  7.2 0.0 reduce-scatter.7.cloned.1.call-start
  7.2 8.1 %abs_reduce_fusion = bf16[2,1024]{1,0:T(2,128)(2,1)S(1)} fusion(bf16[1,2,1024,4608]{3,2,1,0:T(8,128)(2,1)} %param.4), kind=kLoop, calls=%fused_computation.4 | loop fusion | flops 18872320 | bytes 18878464 | tf_op jit(solution)/shard_map/reduce_max | solution.py:33
  15.4 0.1 select_reduce_fusion.1
  15.5 41.9 %pmax.7 = f32[2,3]{0,1:T(4,128)S(1)} all-reduce(f32[2,3]{0,1:T(4,128)S(1)} %select_reduce_fusion.1), channel_id=1, replica_groups=mesh['rep'=4,'fsdp'=8] {'rep','fsdp'}, use_global_device_ids=true, to_apply=%region_2.3 | all-reduce | flops 6 | bytes 48 | tf_op jit(solution)/shard_map/pmax | solution.py:35
  57.4 0.1 select_reduce_fusion
  57.5 12.4 %fusion.1 = bf16[2,1024,4608]{2,1,0:T(8,128)(2,1)S(1)} fusion(bf16[1,2,1024,4608]{3,2,1,0:T(8,128)(2,1)} %param.4, f32[2,1024]{1,0:T(2,128)S(1)} %select_reduce_fusion), kind=kLoop, calls=%fused_computation.2 | loop fusion | flops 37748736 | bytes 37756928 | tf_op jit(solution)/shard_map/convert_element_type | solution.py:38
  69.9 6.8 %slice_bitcast_fusion.1 = (bf16[1024,4608]{1,0:T(8,128)(2,1)}, bf16[1024,4608]{1,0:T(8,128)(2,1)}) fusion(bf16[2,1024,4608]{2,1,0:T(8,128)(2,1)S(1)} %fusion.1), kind=kLoop, calls=%fused_computation.6 | loop fusion | bytes 37748736 | tf_op jit(solution)/shard_map/squeeze | solution.py:46
  76.7 12.7 %copy.5 = bf16[1024,4608]{0,1:T(8,128)(2,1)} copy(bf16[1024,4608]{1,0:T(8,128)(2,1)} %get-tuple-element.4) | data formatting | bytes 18874368
  89.4 0.0 reduce-scatter.7.cloned.1.call-update
  89.4 0.0 reduce-scatter.9.cloned.1.call-start
  89.5 12.4 %copy.7 = bf16[1024,4608]{0,1:T(8,128)(2,1)} copy(bf16[1024,4608]{1,0:T(8,128)(2,1)} %get-tuple-element.5) | data formatting | bytes 18874368
  101.9 0.0 all-gather.3.cloned.1.call-start
  102.0 82.3 %reduce-scatter.7.cloned.1.call-done = bf16[1152,1024]{1,0:T(8,128)(2,1)} async-done(((bf16[4608,1024]{1,0:T(8,128)(2,1)}), bf16[1152,1024]{1,0:T(8,128)(2,1)}) %reduce-scatter.7.cloned.1.call-update) | async-done | bytes 2359312
  184.3 3.0 copy.6
  187.3 95.6 %reduce-scatter.9.cloned.1.call-done = bf16[1152,1024]{1,0:T(8,128)(2,1)} async-done(((bf16[4608,1024]{1,0:T(8,128)(2,1)}), bf16[1152,1024]{1,0:T(8,128)(2,1)}) %reduce-scatter.9.cloned.1.call-update) | async-done | bytes 2359312
  282.9 4.3 copy.8
  287.2 10.1 %fusion.3 = (bf16[1024,1152]{1,0:T(8,128)(2,1)}, bf16[1024,1152]{1,0:T(8,128)(2,1)}, f32[1,1024,1152]{2,1,0:T(8,128)}, f32[1,1024,1152]{2,1,0:T(8,128)}) fusion(bf16[1024,1152]{1,0:T(8,128)(2,1)S(1)} %copy.6, f32[2,1024,1152]{2,1,0:T(8,128)} %param.5, bf16[2,1024,4608]{2,1,0:T(8,128)(2,1)} %param.3, s32[]{:T(128)S(6)} %select_n.11, f32[1024]{0:T(1024)S(1)} %bitcast.47, ...), kind=kLoop, calls=%fused_computation.11 | loop fusion | flops 25952256 | bytes 33038344 | tf_op jit(solution)/shard_map/convert_element_type | solution.py:21
  297.3 0.0 all-gather.3.cloned.1.call-update
  297.3 0.0 all-gather.5.cloned.1.call-start
  297.4 0.5 all-gather.5.cloned.1.call-update
  297.9 9.0 %pad_maximum_fusion.1 = f32[2,1024,1152]{2,1,0:T(8,128)} fusion(f32[1,1024,1152]{2,1,0:T(8,128)} %get-tuple-element.6, f32[1,1024,1152]{2,1,0:T(8,128)} %get-tuple-element.7), kind=kLoop, calls=%fused_computation.7 | loop fusion | flops 2359296 | bytes 18874368 | tf_op jit(solution)/shard_map/stack | solution.py:55
  306.9 86.8 %all-gather.3.cloned.1.call-done = bf16[1024,4608]{1,0:T(8,128)(2,1)} async-done(((bf16[1024,1152]{1,0:T(8,128)(2,1)}), bf16[1024,4608]{1,0:T(8,128)(2,1)}) %all-gather.3.cloned.1.call-update) | async-done | bytes 9437200 | tf_op jit(solution)/shard_map/all_gather | solution.py:52
  393.7 97.9 %all-gather.5.cloned.1.call-done = bf16[1024,4608]{1,0:T(8,128)(2,1)} async-done(((bf16[1024,1152]{1,0:T(8,128)(2,1)}), bf16[1024,4608]{1,0:T(8,128)(2,1)}) %all-gather.5.cloned.1.call-update) | async-done | bytes 9437200 | tf_op jit(solution)/shard_map/all_gather | solution.py:52
  491.6 16.5 %pad_maximum_fusion = bf16[2,1024,4608]{2,1,0:T(8,128)(2,1)} fusion(bf16[1,1024,4608]{2,1,0:T(8,128)(2,1)} %bitcast.44, bf16[1,1024,4608]{2,1,0:T(8,128)(2,1)} %bitcast.43), kind=kLoop, calls=%fused_computation.3 | loop fusion | flops 9437184 | bytes 37748736 | tf_op jit(solution)/shard_map/stack | solution.py:54
  (6 shorter events, 0.1 us)
Async XLA Ops:
  7.2 177.1 %reduce-scatter.7.cloned.1.call-start = ((), (), s32[]{:S(2)}) async-start(), calls=%async_computation.4 | async-start | bytes 11796480
  89.4 193.5 %reduce-scatter.9.cloned.1.call-start = ((), (), s32[]{:S(2)}) async-start(), calls=%async_computation.5 | async-start | bytes 11796480
  101.9 291.8 %all-gather.3.cloned.1.call-start = ((), (), s32[]{:S(2)}) async-start(), calls=%async_computation.2 | async-start | bytes 11796480 | tf_op jit(solution)/shard_map/all_gather | solution.py:52
  297.3 194.3 %all-gather.5.cloned.1.call-start = ((), (), s32[]{:S(2)}) async-start(), calls=%async_computation.3 | async-start | bytes 11796480 | tf_op jit(solution)/shard_map/all_gather | solution.py:52
Sparse Core Ops, SparseCore 0:
  89.5 94.7 reduce-scatter.6
  188.0 94.8 reduce-scatter.8
  297.4 96.2 all-gather.2
  395.4 96.1 all-gather.4
where the time goes:
time: 516 us; the launch traced here: 515 us
  waiting for transfers between devices  363 us (70%)
  other arithmetic  56.4 us (11%)
  blocking collectives  41.9 us (8%)
  local copies, waits for them, and re-layouts  39.2 us (8%)
  between operations  13.8 us (3%)
    all_gather x2, waiting for transfers between devices, on_device(): gathered_layers.append(lax.all_gather(fresh, 'rep', axis=1, tiled=True))  185 us
    unnamed x6, waiting for transfers between devices  178 us
    pmax x1, blocking collectives, on_device(): peak = lax.pmax(local_peak, ('rep', 'fsdp'))  41.9 us
    unnamed x4, local copies, waits for them, and re-layouts  32.4 us
    another operation x1, other arithmetic, on_device(): new_params = jnp.stack(gathered_layers, axis=0)  16.5 us
    convert_element_type x1, other arithmetic, on_device(): jnp.clip(local.astype(jnp.float32) / tau[..., None], -1.0, 1.0)  12.4 us
  transfers between devices with their start and end apart: 4, of which 4 were waited for; matrix products, arithmetic and copies ran while one was open for 5% of the time, Pallas kernels for 0%

commit v1 on v0

v1 whole, which is shorter than its diff:
```python
import functools

import jax
import jax.numpy as jnp
from jax import lax
from jax.experimental import pallas as pl
from jax.experimental.pallas import tpu as pltpu
from jax.sharding import PartitionSpec as P

Q_ROWS = 4096
KV_ROWS = 2048


clip_share = 0.5
peak_eps = 1e-06
outer_rate = 0.7
momentum_decay = 0.9

MESH = pl.DeviceIdType.MESH
CHUNKS_PER_LAYER = 4
EARLY_CHUNKS = 3
STEP_ROWS = 16

Y_OWN, Y_RELAY, X_OWN, X_RELAY = range(4)


def tensor_of(shard, shard_rows):
    row = shard * shard_rows
    return (row >= Q_ROWS).astype(jnp.int32) + (row >= Q_ROWS + KV_ROWS).astype(jnp.int32)


def kernel(
    layers, fsdp, params, deltas, moment, new_params, new_moment,
    local, raw, sum_out, sum_in, fresh, fresh_moment,
    peak, peak_in, group_peak, group_peak_in, tau,
    load_sem, store_sem, raw_send, raw_recv, sum_send, sum_recv,
    own_send, own_recv, relay_send, relay_recv,
    peak_send, peak_recv, group_send, group_recv,
):
    rows, width = moment.shape
    chunks = layers * CHUNKS_PER_LAYER
    chunk = rows // chunks
    half = chunk // 2
    layer_rows = rows // layers
    me = lax.axis_index("rep")
    shard = lax.axis_index("fsdp")
    y, x = me // 2, me % 2
    over_x = y * 2 + (1 - x)
    over_y = (1 - y) * 2 + x
    diagonal = (1 - y) * 2 + (1 - x)
    blocks = (me, over_x, over_y, diagonal)

    def columns(block):
        return pl.ds(pl.multiple_of(block * width, 128), width)

    def whole(c):
        return pl.ds(pl.multiple_of(c * chunk, STEP_ROWS), chunk)

    def first(c):
        return pl.ds(pl.multiple_of(c * chunk, STEP_ROWS), half)

    def second(c):
        return pl.ds(pl.multiple_of(c * chunk + half, STEP_ROWS), half)

    def packed(c):
        return pl.ds(pl.multiple_of(c * half, STEP_ROWS), half)

    def remote(src, dst, send, recv, axis, target):
        return pltpu.make_async_remote_copy(
            src_ref=src, dst_ref=dst, send_sem=send, recv_sem=recv,
            device_id={axis: target}, device_id_type=MESH,
        )

    loads = []
    for layer in range(layers):
        span = pl.ds(layer * layer_rows, layer_rows)
        for slot, block in enumerate(blocks):
            loads.append(
                pltpu.make_async_copy(
                    deltas.at[span, columns(block)], local.at[slot, span], load_sem.at[layer * 4 + slot]
                )
            )
    load_params = pltpu.make_async_copy(params.at[:, columns(me)], fresh, load_sem.at[layers * 4])
    load_moment = pltpu.make_async_copy(moment, fresh_moment, load_sem.at[layers * 4 + 1])
    for load in loads:
        load.start()

    barrier = pltpu.get_barrier_semaphore()
    for step in range(1, fsdp):
        pl.semaphore_signal(
            barrier, inc=1, device_id={"fsdp": lax.rem(shard + step, fsdp)}, device_id_type=MESH
        )
    for block in blocks[1:]:
        pl.semaphore_signal(barrier, inc=1, device_id={"rep": block}, device_id_type=MESH)
    pl.semaphore_wait(barrier, fsdp - 1 + 3)

    def raw_copy(kind, c):
        target = over_y if kind in (Y_OWN, Y_RELAY) else over_x
        span = first(c) if kind in (Y_OWN, Y_RELAY) else second(c)
        block = diagonal if kind in (Y_RELAY, X_RELAY) else target
        return remote(
            deltas.at[span, columns(block)], raw.at[kind, packed(c)],
            raw_send.at[kind, c], raw_recv.at[kind, c], "rep", target,
        )

    def sum_copy(link, c):
        return remote(
            sum_out.at[link, packed(c)], sum_in.at[link, packed(c)],
            sum_send.at[link, c], sum_recv.at[link, c], "rep", over_x if link == 0 else over_y,
        )

    def own_copy(link, c):
        return remote(
            fresh.at[whole(c)], new_params.at[whole(c), columns(me)],
            own_send.at[link, c], own_recv.at[link, c], "rep", over_x if link == 0 else over_y,
        )

    def relay_copy(link, c):
        piece = (second(c), columns(over_y)) if link == 0 else (first(c), columns(over_x))
        return remote(
            new_params.at[piece], new_params.at[piece],
            relay_send.at[link, c], relay_recv.at[link, c], "rep", over_x if link == 0 else over_y,
        )

    def start_raw(c, carry):
        for kind in (Y_RELAY, X_RELAY, Y_OWN, X_OWN):
            raw_copy(kind, c).start()
        return carry

    lax.fori_loop(0, EARLY_CHUNKS, start_raw, 0)

    for layer in range(layers):
        for slot in range(4):
            loads[layer * 4 + slot].wait()

        def largest(i, top):
            span = pl.ds(pl.multiple_of(layer * layer_rows + i * STEP_ROWS, STEP_ROWS), STEP_ROWS)
            for slot in range(4):
                top = jnp.maximum(top, jnp.abs(local[slot, span, :]))
            return top

        top = lax.fori_loop(
            0, layer_rows // STEP_ROWS, largest, jnp.zeros((STEP_ROWS, width), local.dtype)
        ).astype(jnp.float32)
        top = functools.reduce(
            jnp.maximum, [top[:, k * 128 : (k + 1) * 128] for k in range(width // 128)]
        )
        peak[layer] = jnp.maximum(top[:8], top[8:])

    def peak_copy(step):
        return remote(
            peak, peak_in.at[step - 1], peak_send.at[step - 1], peak_recv.at[step - 1],
            "fsdp", lax.rem(shard + step, fsdp),
        )

    for step in range(1, fsdp):
        peak_copy(step).start()
    load_params.start()
    load_moment.start()
    mine = tensor_of(shard, layer_rows)
    for layer in range(layers):
        group_peak[layer] = peak[layer]
    for step in range(1, fsdp):
        peak_copy(step).wait_recv()
        same = tensor_of(lax.rem(shard + fsdp - step, fsdp), layer_rows) == mine
        share = jnp.where(same, jnp.float32(1.0), jnp.float32(0.0))
        for layer in range(layers):
            group_peak[layer] = jnp.maximum(group_peak[layer], peak_in[step - 1, layer] * share)

    def group_copy(slot):
        return remote(
            group_peak, group_peak_in.at[slot], group_send.at[slot], group_recv.at[slot],
            "rep", blocks[slot + 1],
        )

    for slot in range(3):
        group_copy(slot).start()
    lax.fori_loop(EARLY_CHUNKS, chunks, start_raw, 0)
    for slot in range(3):
        group_copy(slot).wait_recv()
    for layer in range(layers):
        top = group_peak[layer]
        for slot in range(3):
            top = jnp.maximum(top, group_peak_in[slot, layer])
        top = jnp.max(jnp.max(top, axis=0, keepdims=True), axis=1, keepdims=True)
        tau[layer] = jnp.broadcast_to(clip_share * (top + peak_eps), tau.shape[1:])

    def code(values, scale):
        return jnp.clip(values.astype(jnp.float32) / scale, -1.0, 1.0).astype(jnp.bfloat16).astype(jnp.float32)

    def relay_sums(c, carry):
        layer = c // CHUNKS_PER_LAYER
        for link, kind in ((0, Y_RELAY), (1, X_RELAY)):
            raw_copy(kind, c).wait_recv()
            start = c * chunk + link * half

            def add(i, inner):
                here = pl.ds(pl.multiple_of(start + i * STEP_ROWS, STEP_ROWS), STEP_ROWS)
                there = pl.ds(pl.multiple_of(c * half + i * STEP_ROWS, STEP_ROWS), STEP_ROWS)
                scale = tau[layer]
                total = code(local[1 + link, here, :], scale) + code(raw[kind, there, :], scale)
                sum_out[link, there, :] = total.astype(jnp.bfloat16)
                return inner

            lax.fori_loop(0, half // STEP_ROWS, add, 0)
            sum_copy(link, c).start()
        return carry

    lax.fori_loop(0, chunks, relay_sums, 0)

    load_params.wait()
    load_moment.wait()

    def store_params(c):
        return pltpu.make_async_copy(
            fresh.at[whole(c)], new_params.at[whole(c), columns(me)], store_sem.at[0, c]
        )

    def store_moment(c):
        return pltpu.make_async_copy(
            fresh_moment.at[whole(c)], new_moment.at[whole(c)], store_sem.at[1, c]
        )

    def update(c, carry):
        layer = c // CHUNKS_PER_LAYER
        for link, kind in ((0, Y_OWN), (1, X_OWN)):
            raw_copy(kind, c).wait_recv()
            sum_copy(link, c).wait_recv()
            start = c * chunk + link * half

            def apply(i, inner):
                here = pl.ds(pl.multiple_of(start + i * STEP_ROWS, STEP_ROWS), STEP_ROWS)
                there = pl.ds(pl.multiple_of(c * half + i * STEP_ROWS, STEP_ROWS), STEP_ROWS)
                scale = tau[layer]
                total = code(local[0, here, :], scale) + code(raw[kind, there, :], scale)
                total = total + sum_in[link, there, :].astype(jnp.float32)
                outer = scale * total / jnp.float32(4)
                moved = momentum_decay * fresh_moment[here, :] + outer
                fresh_moment[here, :] = moved
                fresh[here, :] = (
                    fresh[here, :].astype(jnp.float32) - outer_rate * (outer + momentum_decay * moved)
                ).astype(jnp.bfloat16)
                return inner

            lax.fori_loop(0, half // STEP_ROWS, apply, 0)
        own_copy(0, c).start()
        own_copy(1, c).start()
        store_params(c).start()
        store_moment(c).start()
        return carry

    lax.fori_loop(0, chunks, update, 0)

    def relay(c, carry):
        own_copy(0, c).wait_recv()
        relay_copy(1, c).start()
        own_copy(1, c).wait_recv()
        relay_copy(0, c).start()
        return carry

    lax.fori_loop(0, chunks, relay, 0)

    def drain(c, carry):
        for kind in range(4):
            raw_copy(kind, c).wait_send()
        store_params(c).wait()
        store_moment(c).wait()
        for link in range(2):
            sum_copy(link, c).wait_send()
            own_copy(link, c).wait_send()
            relay_copy(link, c).wait()
        return carry

    for step in range(1, fsdp):
        peak_copy(step).wait_send()
    for slot in range(3):
        group_copy(slot).wait_send()
    lax.fori_loop(0, chunks, drain, 0)


def on_device(rep, fsdp, params, deltas, momentum):
    layers, shard_rows, depth = params.shape
    width = momentum.shape[2]
    rows = layers * shard_rows
    chunks = layers * CHUNKS_PER_LAYER
    assert rep == 4 and width * rep == depth and width % 128 == 0
    assert Q_ROWS % shard_rows == 0 and KV_ROWS % shard_rows == 0
    assert shard_rows % (CHUNKS_PER_LAYER * 2 * STEP_ROWS) == 0
    dma = pltpu.SemaphoreType.DMA
    hbm = pl.BlockSpec(memory_space=pl.ANY)
    new_params, new_momentum = pl.pallas_call(
        functools.partial(kernel, layers, fsdp),
        out_shape=(
            jax.ShapeDtypeStruct((rows, depth), params.dtype),
            jax.ShapeDtypeStruct((rows, width), momentum.dtype),
        ),
        in_specs=[hbm] * 3,
        out_specs=(hbm, hbm),
        scratch_shapes=[
            pltpu.VMEM((4, rows, width), deltas.dtype),
            pltpu.VMEM((4, rows // 2, width), deltas.dtype),
            pltpu.VMEM((2, rows // 2, width), jnp.bfloat16),
            pltpu.VMEM((2, rows // 2, width), jnp.bfloat16),
            pltpu.VMEM((rows, width), params.dtype),
            pltpu.VMEM((rows, width), momentum.dtype),
            pltpu.VMEM((layers, 8, 128), jnp.float32),
            pltpu.VMEM((fsdp - 1, layers, 8, 128), jnp.float32),
            pltpu.VMEM((layers, 8, 128), jnp.float32),
            pltpu.VMEM((3, layers, 8, 128), jnp.float32),
            pltpu.VMEM((layers, STEP_ROWS, width), jnp.float32),
            dma((layers * 4 + 2,)),
            dma((2, chunks)),
            dma((4, chunks)),
            dma((4, chunks)),
            dma((2, chunks)),
            dma((2, chunks)),
            dma((2, chunks)),
            dma((2, chunks)),
            dma((2, chunks)),
            dma((2, chunks)),
            dma((fsdp - 1,)),
            dma((fsdp - 1,)),
            dma((3,)),
            dma((3,)),
        ],
        compiler_params=pltpu.CompilerParams(
            collective_id=0, has_side_effects=True, vmem_limit_bytes=60 * 1024 * 1024
        ),
        name="outer_step",
    )(
        params.reshape(rows, depth),
        deltas.reshape(rows, depth),
        momentum.reshape(rows, width),
    )
    return (
        new_params.reshape(params.shape),
        new_momentum.reshape(momentum.shape),
    )


def solution(mesh):
    placed = (P(None, "fsdp", None), P("rep", None, "fsdp", None), P(None, "fsdp", "rep"))
    return jax.shard_map(
        functools.partial(on_device, mesh.shape["rep"], mesh.shape["fsdp"]),
        mesh=mesh,
        in_specs=placed,
        out_specs=(P(None, "fsdp", None), P(None, "fsdp", "rep")),
        check_vma=False,
    )
```

time: 516 us -> 335 us (0.65)
  waiting for transfers between devices: 363 us -> 0 us
  Pallas kernels: 0 us -> 313 us
  other arithmetic: 56.4 us -> 0 us
  blocking collectives: 41.9 us -> 0 us
  local copies, waits for them, and re-layouts: 39.2 us -> 20.8 us
  between operations: 13.8 us -> 0.65 us
    pallas_call x0 -> x1, Pallas kernels: none -> 313 us  [on_device(): pl.pallas_call(functools.partial(kernel, layers, fsdp), out_shape=(jax.Sh...]
    all_gather x2 -> x0, waiting for transfers between devices: 185 us -> none  [on_device(): gathered_layers.append(lax.all_gather(fresh, 'rep', axis=1, tiled=True))]
    unnamed x6 -> x0, waiting for transfers between devices: 178 us -> none
    pmax x1 -> x0, blocking collectives: 41.9 us -> none  [on_device(): peak = lax.pmax(local_peak, ('rep', 'fsdp'))]
    another operation x2 -> x0, other arithmetic: 25.6 us -> none  [the longest x1 16.5 us: on_device(): new_params = jnp.stack(gathered_layers, axis=0)]
    convert_element_type x3 -> x0, other arithmetic: 22.5 us -> none  [the longest x1 12.4 us: on_device(): jnp.clip(local.astype(jnp.float32) / tau[..., None], -1.0, 1.0)]
    unnamed x4, local copies, waits for them, and re-layouts: 32.4 us -> 20.8 us
    reduce_max x2 -> x0, other arithmetic: 8.21 us -> none  [the longest x1 8.11 us: on_device(): row_peak = jnp.max(jnp.abs(local), axis=2).astype(jnp.float32)]
  transfers between devices with their start and end apart: 4 -> 0, of which waited for: 4 -> 0; matrix products, arithmetic and copies ran while one was open for 5% -> 0% of each run, Pallas kernels for 0% -> 0%
where the time goes in v1:
time: 335 us
  Pallas kernels  313 us (93%)
  local copies, waits for them, and re-layouts  20.8 us (6%)
    pallas_call x1, Pallas kernels, on_device(): pl.pallas_call(functools.partial(kernel, layers, fsdp), out_shape=(jax.Sh...  313 us
    unnamed x4, local copies, waits for them, and re-layouts  20.8 us

profile of v1, /device:TPU:0, one launch (start us, length us, event | category | flops | bytes accessed | tf_op | source)
XLA Modules:
  0.0 335.0 jit_solution(4664800767506408749)
XLA Ops:
  0.6 313.5 %outer_step.1 = (bf16[2048,4608]{1,0:T(8,128)(2,1)}, f32[2048,1152]{1,0:T(8,128)}) custom-call(bf16[2048,4608]{1,0:T(8,128)(2,1)} %bitcast.6, bf16[2048,4608]{1,0:T(8,128)(2,1)} %bitcast.7, f32[2048,1152]{1,0:T(8,128)} %bitcast.9), custom_call_target="tpu_custom_call" | custom-call | tf_op jit(solution)/shard_map/outer_step/pallas_call | solution.py:291
  314.1 0.0 copy-start
  314.1 17.1 %copy.7 = bf16[2,1024,4608]{2,1,0:T(8,128)(2,1)} copy(bf16[2,1024,4608]{2,1,0:T(8,128)(2,1)} %bitcast.5) | data formatting | bytes 37748736
  331.2 0.0 copy-done
  331.2 3.7 %copy.8 = f32[2,1024,1152]{2,1,0:T(8,128)} copy(f32[2,1024,1152]{2,1,0:T(8,128)S(1)} %bitcast.8) | data formatting | bytes 18874368
Async XLA Ops:
  314.1 17.1 %copy-start = (f32[2048,1152]{1,0:T(8,128)S(1)}, f32[2048,1152]{1,0:T(8,128)}, u32[]{:S(2)}) copy-start(f32[2048,1152]{1,0:T(8,128)} %get-tuple-element.5) | copy-start | bytes 28311556

commit v2 on v1

--- a/solution.py
+++ b/solution.py
@@ -31,9 +31,9 @@
 
 def kernel(
     layers, fsdp, params, deltas, moment, new_params, new_moment,
-    local, raw, sum_out, sum_in, fresh, fresh_moment,
+    local, raw, sum_out, sum_in,
     peak, peak_in, group_peak, group_peak_in, tau,
-    load_sem, store_sem, raw_send, raw_recv, sum_send, sum_recv,
+    load_sem, raw_send, raw_recv, sum_send, sum_recv,
     own_send, own_recv, relay_send, relay_recv,
     peak_send, peak_recv, group_send, group_recv,
 ):
@@ -77,11 +77,13 @@
         for slot, block in enumerate(blocks):
             loads.append(
                 pltpu.make_async_copy(
-                    deltas.at[span, columns(block)], local.at[slot, span], load_sem.at[layer * 4 + slot]
+                    deltas.at[span, columns(block)],
+                    local.at[slot, span] if slot < 3 else new_params.at[diagonal, span],
+                    load_sem.at[layer * 4 + slot],
                 )
             )
-    load_params = pltpu.make_async_copy(params.at[:, columns(me)], fresh, load_sem.at[layers * 4])
-    load_moment = pltpu.make_async_copy(moment, fresh_moment, load_sem.at[layers * 4 + 1])
+    load_params = pltpu.make_async_copy(params.at[:, columns(me)], new_params.at[me], load_sem.at[layers * 4])
+    load_moment = pltpu.make_async_copy(moment, new_moment, load_sem.at[layers * 4 + 1])
     for load in loads:
         load.start()
 
@@ -111,12 +113,12 @@
 
     def own_copy(link, c):
         return remote(
-            fresh.at[whole(c)], new_params.at[whole(c), columns(me)],
+            new_params.at[me, whole(c)], new_params.at[me, whole(c)],
             own_send.at[link, c], own_recv.at[link, c], "rep", over_x if link == 0 else over_y,
         )
 
     def relay_copy(link, c):
-        piece = (second(c), columns(over_y)) if link == 0 else (first(c), columns(over_x))
+        piece = (over_y, second(c)) if link == 0 else (over_x, first(c))
         return remote(
             new_params.at[piece], new_params.at[piece],
             relay_send.at[link, c], relay_recv.at[link, c], "rep", over_x if link == 0 else over_y,
@@ -135,9 +137,9 @@
 
         def largest(i, top):
             span = pl.ds(pl.multiple_of(layer * layer_rows + i * STEP_ROWS, STEP_ROWS), STEP_ROWS)
-            for slot in range(4):
+            for slot in range(3):
                 top = jnp.maximum(top, jnp.abs(local[slot, span, :]))
-            return top
+            return jnp.maximum(top, jnp.abs(new_params[diagonal, span, :]))
 
         top = lax.fori_loop(
             0, layer_rows // STEP_ROWS, largest, jnp.zeros((STEP_ROWS, width), local.dtype)
@@ -211,16 +213,6 @@
     load_params.wait()
     load_moment.wait()
 
-    def store_params(c):
-        return pltpu.make_async_copy(
-            fresh.at[whole(c)], new_params.at[whole(c), columns(me)], store_sem.at[0, c]
-        )
-
-    def store_moment(c):
-        return pltpu.make_async_copy(
-            fresh_moment.at[whole(c)], new_moment.at[whole(c)], store_sem.at[1, c]
-        )
-
     def update(c, carry):
         layer = c // CHUNKS_PER_LAYER
         for link, kind in ((0, Y_OWN), (1, X_OWN)):
@@ -235,18 +227,16 @@
                 total = code(local[0, here, :], scale) + code(raw[kind, there, :], scale)
                 total = total + sum_in[link, there, :].astype(jnp.float32)
                 outer = scale * total / jnp.float32(4)
-                moved = momentum_decay * fresh_moment[here, :] + outer
-                fresh_moment[here, :] = moved
-                fresh[here, :] = (
-                    fresh[here, :].astype(jnp.float32) - outer_rate * (outer + momentum_decay * moved)
+                moved = momentum_decay * new_moment[here, :] + outer
+                new_moment[here, :] = moved
+                new_params[me, here, :] = (
+                    new_params[me, here, :].astype(jnp.float32) - outer_rate * (outer + momentum_decay * moved)
                 ).astype(jnp.bfloat16)
                 return inner
 
             lax.fori_loop(0, half // STEP_ROWS, apply, 0)
         own_copy(0, c).start()
         own_copy(1, c).start()
-        store_params(c).start()
-        store_moment(c).start()
         return carry
 
     lax.fori_loop(0, chunks, update, 0)
@@ -263,8 +253,6 @@
     def drain(c, carry):
         for kind in range(4):
             raw_copy(kind, c).wait_send()
-        store_params(c).wait()
-        store_moment(c).wait()
         for link in range(2):
             sum_copy(link, c).wait_send()
             own_copy(link, c).wait_send()
@@ -276,6 +264,19 @@
     for slot in range(3):
         group_copy(slot).wait_send()
     lax.fori_loop(0, chunks, drain, 0)
+
+
+def store_outputs(blocks, fresh_moment, new_params, new_moment, sems):
+    count, _, width = blocks.shape
+    stores = [
+        pltpu.make_async_copy(blocks.at[k], new_params.at[:, pl.ds(k * width, width)], sems.at[k])
+        for k in range(count)
+    ]
+    stores.append(pltpu.make_async_copy(fresh_moment, new_moment, sems.at[count]))
+    for store in stores:
+        store.start()
+    for store in stores:
+        store.wait()
 
 
 def on_device(rep, fsdp, params, deltas, momentum):
@@ -286,30 +287,30 @@
     assert rep == 4 and width * rep == depth and width % 128 == 0
     assert Q_ROWS % shard_rows == 0 and KV_ROWS % shard_rows == 0
     assert shard_rows % (CHUNKS_PER_LAYER * 2 * STEP_ROWS) == 0
+    block_bytes = rows * width * 2
+    kernel_bytes = block_bytes * 7 + (2 << 20)
     dma = pltpu.SemaphoreType.DMA
     hbm = pl.BlockSpec(memory_space=pl.ANY)
-    new_params, new_momentum = pl.pallas_call(
+    vmem = pl.BlockSpec(memory_space=pltpu.VMEM)
+    blocks, fresh_moment = pl.pallas_call(
         functools.partial(kernel, layers, fsdp),
         out_shape=(
-            jax.ShapeDtypeStruct((rows, depth), params.dtype),
-            jax.ShapeDtypeStruct((rows, width), momentum.dtype),
+            pltpu.VMEM((rep, rows, width), params.dtype),
+            pltpu.VMEM((rows, width), momentum.dtype),
         ),
         in_specs=[hbm] * 3,
-        out_specs=(hbm, hbm),
+        out_specs=(vmem, vmem),
         scratch_shapes=[
-            pltpu.VMEM((4, rows, width), deltas.dtype),
+            pltpu.VMEM((3, rows, width), deltas.dtype),
             pltpu.VMEM((4, rows // 2, width), deltas.dtype),
             pltpu.VMEM((2, rows // 2, width), jnp.bfloat16),
             pltpu.VMEM((2, rows // 2, width), jnp.bfloat16),
-            pltpu.VMEM((rows, width), params.dtype),
-            pltpu.VMEM((rows, width), momentum.dtype),
             pltpu.VMEM((layers, 8, 128), jnp.float32),
             pltpu.VMEM((fsdp - 1, layers, 8, 128), jnp.float32),
             pltpu.VMEM((layers, 8, 128), jnp.float32),
             pltpu.VMEM((3, layers, 8, 128), jnp.float32),
             pltpu.VMEM((layers, STEP_ROWS, width), jnp.float32),
             dma((layers * 4 + 2,)),
-            dma((2, chunks)),
             dma((4, chunks)),
             dma((4, chunks)),
             dma((2, chunks)),
@@ -324,13 +325,28 @@
             dma((3,)),
         ],
         compiler_params=pltpu.CompilerParams(
-            collective_id=0, has_side_effects=True, vmem_limit_bytes=60 * 1024 * 1024
+            collective_id=0, has_side_effects=True, vmem_limit_bytes=kernel_bytes
         ),
         name="outer_step",
     )(
         params.reshape(rows, depth),
         deltas.reshape(rows, depth),
         momentum.reshape(rows, width),
+    )
+    new_params, new_momentum = pl.pallas_call(
+        store_outputs,
+        out_shape=(
+            jax.ShapeDtypeStruct((rows, depth), params.dtype),
+            jax.ShapeDtypeStruct((rows, width), momentum.dtype),
+        ),
+        in_specs=[vmem] * 2,
+        out_specs=(hbm, hbm),
+        scratch_shapes=[dma((rep + 1,))],
+        compiler_params=pltpu.CompilerParams(vmem_limit_bytes=1 << 20),
+        name="store_outputs",
+    )(
+        pltpu.with_memory_space_constraint(blocks, pltpu.VMEM),
+        pltpu.with_memory_space_constraint(fresh_moment, pltpu.VMEM),
     )
     return (
         new_params.reshape(params.shape),

time: 335 us -> 324 us (0.967)
  local copies, waits for them, and re-layouts: 20.8 us -> 0 us
  Pallas kernels: 313 us -> 323 us
    unnamed x4 -> x0, local copies, waits for them, and re-layouts: 20.8 us -> none
    pallas_call x1 -> x2, Pallas kernels: 313 us -> 323 us  [the longest x1 313 us: on_device(): pl.pallas_call(functools.partial(kernel, layers, fsdp), out_shape=(pltpu....]
where the time goes in v2:
time: 324 us; the launch traced here: 323 us
  Pallas kernels  323 us (100%)
    pallas_call x1, Pallas kernels, on_device(): pl.pallas_call(functools.partial(kernel, layers, fsdp), out_shape=(pltpu....  313 us
    pallas_call x1, Pallas kernels, on_device(): pl.pallas_call(store_outputs, out_shape=(jax.ShapeDtypeStruct((rows, dept...  9.6 us

profile of v2, /device:TPU:0, one launch (start us, length us, event | category | flops | bytes accessed | tf_op | source)
XLA Modules:
  0.0 323.5 jit_solution(11561518459424746825)
XLA Ops:
  0.6 313.3 %outer_step.1 = (bf16[4,2048,1152]{2,1,0:T(8,128)(2,1)S(1)}, f32[2048,1152]{1,0:T(8,128)S(1)}) custom-call(bf16[2048,4608]{1,0:T(8,128)(2,1)} %bitcast.5, bf16[2048,4608]{1,0:T(8,128)(2,1)} %bitcast.6, f32[2048,1152]{1,0:T(8,128)} %bitcast.7), custom_call_target="tpu_custom_call" | custom-call | tf_op jit(solution)/shard_map/outer_step/pallas_call | solution.py:295
  313.9 9.6 %store_outputs.1 = (bf16[2048,4608]{1,0:T(8,128)(2,1)}, f32[2048,1152]{1,0:T(8,128)}) custom-call(bf16[4,2048,1152]{2,1,0:T(8,128)(2,1)S(1)} %get-tuple-element.6.blocks, f32[2048,1152]{1,0:T(8,128)S(1)} %get-tuple-element.7.fresh_moment), custom_call_target="tpu_custom_call" | custom-call | tf_op jit(solution)/shard_map/store_outputs/pallas_call | solution.py:336

commit v3 on v2

--- a/solution.py
+++ b/solution.py
@@ -18,7 +18,7 @@
 
 MESH = pl.DeviceIdType.MESH
 CHUNKS_PER_LAYER = 4
-EARLY_CHUNKS = 3
+EARLY_CHUNKS = 2
 STEP_ROWS = 16
 
 Y_OWN, Y_RELAY, X_OWN, X_RELAY = range(4)
@@ -32,10 +32,10 @@
 def kernel(
     layers, fsdp, params, deltas, moment, new_params, new_moment,
     local, raw, sum_out, sum_in,
-    peak, peak_in, group_peak, group_peak_in, tau,
+    peak, group_peak, group_peak_in, run_peak, run_peak_in, tau,
     load_sem, raw_send, raw_recv, sum_send, sum_recv,
     own_send, own_recv, relay_send, relay_recv,
-    peak_send, peak_recv, group_send, group_recv,
+    group_send, group_recv, run_send, run_recv,
 ):
     rows, width = moment.shape
     chunks = layers * CHUNKS_PER_LAYER
@@ -88,13 +88,19 @@
         load.start()
 
     barrier = pltpu.get_barrier_semaphore()
-    for step in range(1, fsdp):
-        pl.semaphore_signal(
-            barrier, inc=1, device_id={"fsdp": lax.rem(shard + step, fsdp)}, device_id_type=MESH
-        )
-    for block in blocks[1:]:
-        pl.semaphore_signal(barrier, inc=1, device_id={"rep": block}, device_id_type=MESH)
-    pl.semaphore_wait(barrier, fsdp - 1 + 3)
+    for target in (over_x, over_y):
+        pl.semaphore_signal(barrier, inc=1, device_id={"rep": target}, device_id_type=MESH)
+
+    @pl.when(shard > 0)
+    def _():
+        pl.semaphore_signal(barrier, inc=1, device_id={"fsdp": shard - 1}, device_id_type=MESH)
+
+    @pl.when(shard < fsdp - 1)
+    def _():
+        pl.semaphore_signal(barrier, inc=1, device_id={"fsdp": shard + 1}, device_id_type=MESH)
+
+    inner = jnp.where(shard > 0, 1, 0) + jnp.where(shard < fsdp - 1, 1, 0)
+    pl.semaphore_wait(barrier, 2 + inner)
 
     def raw_copy(kind, c):
         target = over_y if kind in (Y_OWN, Y_RELAY) else over_x
@@ -149,41 +155,50 @@
         )
         peak[layer] = jnp.maximum(top[:8], top[8:])
 
-    def peak_copy(step):
-        return remote(
-            peak, peak_in.at[step - 1], peak_send.at[step - 1], peak_recv.at[step - 1],
-            "fsdp", lax.rem(shard + step, fsdp),
-        )
-
-    for step in range(1, fsdp):
-        peak_copy(step).start()
     load_params.start()
     load_moment.start()
+
+    def group_copy(step):
+        return remote(
+            peak if step == 0 else group_peak, group_peak_in.at[step],
+            group_send.at[step], group_recv.at[step], "rep", over_x if step == 0 else over_y,
+        )
+
+    group_copy(0).start()
+    lax.fori_loop(EARLY_CHUNKS, EARLY_CHUNKS + 1, start_raw, 0)
+    group_copy(0).wait_recv()
+    group_peak[...] = jnp.maximum(peak[...], group_peak_in[0])
+    group_copy(1).start()
+    lax.fori_loop(EARLY_CHUNKS + 1, chunks, start_raw, 0)
+    group_copy(1).wait_recv()
+    for way in range(2):
+        run_peak[way] = jnp.maximum(group_peak[...], group_peak_in[1])
+
+    def line_copy(way):
+        return remote(
+            run_peak.at[way], run_peak_in.at[way], run_send.at[way], run_recv.at[way],
+            "fsdp", shard + 1 if way == 0 else shard - 1,
+        )
+
     mine = tensor_of(shard, layer_rows)
+    has_left, has_right = shard > 0, shard < fsdp - 1
+    for way, behind, ahead, before in (
+        (0, has_left, has_right, shard - 1),
+        (1, has_right, has_left, shard + 1),
+    ):
+        share = jnp.where(tensor_of(before, layer_rows) == mine, jnp.float32(1.0), jnp.float32(0.0))
+
+        @pl.when(behind)
+        def _():
+            line_copy(way).wait_recv()
+            run_peak[way] = jnp.maximum(run_peak[way], run_peak_in[way] * share)
+
+        @pl.when(ahead)
+        def _():
+            line_copy(way).start()
+
     for layer in range(layers):
-        group_peak[layer] = peak[layer]
-    for step in range(1, fsdp):
-        peak_copy(step).wait_recv()
-        same = tensor_of(lax.rem(shard + fsdp - step, fsdp), layer_rows) == mine
-        share = jnp.where(same, jnp.float32(1.0), jnp.float32(0.0))
-        for layer in range(layers):
-            group_peak[layer] = jnp.maximum(group_peak[layer], peak_in[step - 1, layer] * share)
-
-    def group_copy(slot):
-        return remote(
-            group_peak, group_peak_in.at[slot], group_send.at[slot], group_recv.at[slot],
-            "rep", blocks[slot + 1],
-        )
-
-    for slot in range(3):
-        group_copy(slot).start()
-    lax.fori_loop(EARLY_CHUNKS, chunks, start_raw, 0)
-    for slot in range(3):
-        group_copy(slot).wait_recv()
-    for layer in range(layers):
-        top = group_peak[layer]
-        for slot in range(3):
-            top = jnp.maximum(top, group_peak_in[slot, layer])
+        top = jnp.maximum(run_peak[0, layer], run_peak[1, layer])
         top = jnp.max(jnp.max(top, axis=0, keepdims=True), axis=1, keepdims=True)
         tau[layer] = jnp.broadcast_to(clip_share * (top + peak_eps), tau.shape[1:])
 
@@ -259,10 +274,14 @@
             relay_copy(link, c).wait()
         return carry
 
-    for step in range(1, fsdp):
-        peak_copy(step).wait_send()
-    for slot in range(3):
-        group_copy(slot).wait_send()
+    for way, ahead in ((0, has_right), (1, has_left)):
+
+        @pl.when(ahead)
+        def _():
+            line_copy(way).wait_send()
+
+    for step in range(2):
+        group_copy(step).wait_send()
     lax.fori_loop(0, chunks, drain, 0)
 
 
@@ -306,9 +325,10 @@
             pltpu.VMEM((2, rows // 2, width), jnp.bfloat16),
             pltpu.VMEM((2, rows // 2, width), jnp.bfloat16),
             pltpu.VMEM((layers, 8, 128), jnp.float32),
-            pltpu.VMEM((fsdp - 1, layers, 8, 128), jnp.float32),
             pltpu.VMEM((layers, 8, 128), jnp.float32),
-            pltpu.VMEM((3, layers, 8, 128), jnp.float32),
+            pltpu.VMEM((2, layers, 8, 128), jnp.float32),
+            pltpu.VMEM((2, layers, 8, 128), jnp.float32),
+            pltpu.VMEM((2, layers, 8, 128), jnp.float32),
             pltpu.VMEM((layers, STEP_ROWS, width), jnp.float32),
             dma((layers * 4 + 2,)),
             dma((4, chunks)),
@@ -319,10 +339,10 @@
             dma((2, chunks)),
             dma((2, chunks)),
             dma((2, chunks)),
-            dma((fsdp - 1,)),
-            dma((fsdp - 1,)),
-            dma((3,)),
-            dma((3,)),
+            dma((2,)),
+            dma((2,)),
+            dma((2,)),
+            dma((2,)),
         ],
         compiler_params=pltpu.CompilerParams(
             collective_id=0, has_side_effects=True, vmem_limit_bytes=kernel_bytes

time: 324 us -> 321 us (level)
  no operation moved by 1% of the time
where the time goes in v3:
time: 321 us
  Pallas kernels  321 us (100%)
    pallas_call x1, Pallas kernels, on_device(): pl.pallas_call(functools.partial(kernel, layers, fsdp), out_shape=(pltpu....  311 us
    pallas_call x1, Pallas kernels, on_device(): pl.pallas_call(store_outputs, out_shape=(jax.ShapeDtypeStruct((rows, dept...  9.6 us

profile of v3, /device:TPU:0, one launch (start us, length us, event | category | flops | bytes accessed | tf_op | source)
XLA Modules:
  0.0 321.2 jit_solution(6242680767484187950)
XLA Ops:
  0.6 310.9 %outer_step.1 = (bf16[4,2048,1152]{2,1,0:T(8,128)(2,1)S(1)}, f32[2048,1152]{1,0:T(8,128)S(1)}) custom-call(bf16[2048,4608]{1,0:T(8,128)(2,1)} %bitcast.5, bf16[2048,4608]{1,0:T(8,128)(2,1)} %bitcast.6, f32[2048,1152]{1,0:T(8,128)} %bitcast.7), custom_call_target="tpu_custom_call" | custom-call | tf_op jit(solution)/shard_map/outer_step/pallas_call | solution.py:314
  311.6 9.6 %store_outputs.1 = (bf16[2048,4608]{1,0:T(8,128)(2,1)}, f32[2048,1152]{1,0:T(8,128)}) custom-call(bf16[4,2048,1152]{2,1,0:T(8,128)(2,1)S(1)} %get-tuple-element.6.blocks, f32[2048,1152]{1,0:T(8,128)S(1)} %get-tuple-element.7.fresh_moment), custom_call_target="tpu_custom_call" | custom-call | tf_op jit(solution)/shard_map/store_outputs/pallas_call | solution.py:356

commit v4 on v3

--- a/solution.py
+++ b/solution.py
@@ -257,10 +257,13 @@
     lax.fori_loop(0, chunks, update, 0)
 
     def relay(c, carry):
-        own_copy(0, c).wait_recv()
-        relay_copy(1, c).start()
-        own_copy(1, c).wait_recv()
-        relay_copy(0, c).start()
+        for link in range(2):
+            own_copy(link, c).wait_recv()
+
+            @pl.when(c < chunks - 1)
+            def _():
+                relay_copy(1 - link, c).start()
+
         return carry
 
     lax.fori_loop(0, chunks, relay, 0)
@@ -271,7 +274,11 @@
         for link in range(2):
             sum_copy(link, c).wait_send()
             own_copy(link, c).wait_send()
-            relay_copy(link, c).wait()
+
+            @pl.when(c < chunks - 1)
+            def _():
+                relay_copy(link, c).wait()
+
         return carry
 
     for way, ahead in ((0, has_right), (1, has_left)):
@@ -293,6 +300,30 @@
     ]
     stores.append(pltpu.make_async_copy(fresh_moment, new_moment, sems.at[count]))
     for store in stores:
+        store.start()
+    for store in stores:
+        store.wait()
+
+
+def store_tail(piece_y, piece_x, _, new_params, staged, sems):
+    rows = new_params.shape[0]
+    half, width = piece_y.shape
+    me = lax.axis_index("rep")
+    diagonal = 3 - me
+    columns = pl.ds(pl.multiple_of(diagonal * width, 128), width)
+    loads = [
+        pltpu.make_async_copy(piece, staged.at[k], sems.at[k]) for k, piece in enumerate((piece_y, piece_x))
+    ]
+    stores = [
+        pltpu.make_async_copy(
+            staged.at[k], new_params.at[pl.ds(rows - (2 - k) * half, half), columns], sems.at[2 + k]
+        )
+        for k in range(2)
+    ]
+    for load in loads:
+        load.start()
+    for load, store in zip(loads, stores):
+        load.wait()
         store.start()
     for store in stores:
         store.wait()
@@ -353,6 +384,15 @@
         deltas.reshape(rows, depth),
         momentum.reshape(rows, width),
     )
+    half = rows // chunks // 2
+    me = lax.axis_index("rep")
+    over_x = me // 2 * 2 + 1 - me % 2
+    over_y = (1 - me // 2) * 2 + me % 2
+    tail = rows - 2 * half
+    piece_y = lax.dynamic_slice(blocks, (over_x, tail, 0), (1, half, width))[0]
+    piece_x = lax.dynamic_slice(blocks, (over_y, tail + half, 0), (1, half, width))[0]
+    piece_y = lax.ppermute(piece_y, "rep", [(k, (k + 2) % 4) for k in range(4)])
+    piece_x = lax.ppermute(piece_x, "rep", [(k, k + 1 - 2 * (k % 2)) for k in range(4)])
     new_params, new_momentum = pl.pallas_call(
         store_outputs,
         out_shape=(
@@ -363,11 +403,22 @@
         out_specs=(hbm, hbm),
         scratch_shapes=[dma((rep + 1,))],
         compiler_params=pltpu.CompilerParams(vmem_limit_bytes=1 << 20),
+        cost_estimate=pl.CostEstimate(flops=0, bytes_accessed=rows * depth * 4, transcendentals=0),
         name="store_outputs",
     )(
         pltpu.with_memory_space_constraint(blocks, pltpu.VMEM),
         pltpu.with_memory_space_constraint(fresh_moment, pltpu.VMEM),
     )
+    new_params = pl.pallas_call(
+        store_tail,
+        out_shape=jax.ShapeDtypeStruct((rows, depth), params.dtype),
+        in_specs=[hbm] * 3,
+        out_specs=hbm,
+        input_output_aliases={2: 0},
+        scratch_shapes=[pltpu.VMEM((2, half, width), params.dtype), dma((4,))],
+        compiler_params=pltpu.CompilerParams(vmem_limit_bytes=4 << 20),
+        name="store_tail",
+    )(piece_y, piece_x, new_params)
     return (
         new_params.reshape(params.shape),
         new_momentum.reshape(momentum.shape),

time: 321 us -> 318 us (level)
  Pallas kernels: 321 us -> 315 us
    pallas_call x1, Pallas kernels: 311 us -> 305 us  [on_device(): pl.pallas_call(functools.partial(kernel, layers, fsdp), out_shape=(pltpu....]
  transfers between devices with their start and end apart: 0 -> 2, of which waited for: 0 -> 0; matrix products, arithmetic and copies ran while one was open for 0% -> 0% of each run, Pallas kernels for 0% -> 3%
where the time goes in v4:
time: 318 us
  Pallas kernels  315 us (99%)
    pallas_call x1, Pallas kernels, on_device(): pl.pallas_call(functools.partial(kernel, layers, fsdp), out_shape=(pltpu....  305 us
    pallas_call x1, Pallas kernels, on_device(): pl.pallas_call(store_outputs, out_shape=(jax.ShapeDtypeStruct((rows, dept...  9.59 us
  transfers between devices with their start and end apart: 2, of which 0 were waited for; matrix products, arithmetic and copies ran while one was open for 0% of the time, Pallas kernels for 3%

profile of v4, /device:TPU:0, one launch (start us, length us, event | category | flops | bytes accessed | tf_op | source)
XLA Modules:
  0.0 318.1 jit_solution(8332111891587996418)
XLA Ops:
  0.7 304.6 %outer_step.1 = (bf16[4,2048,1152]{2,1,0:T(8,128)(2,1)S(1)}, f32[2048,1152]{1,0:T(8,128)S(1)}) custom-call(bf16[2048,4608]{1,0:T(8,128)(2,1)} %bitcast.10, bf16[2048,4608]{1,0:T(8,128)(2,1)} %bitcast.11, f32[2048,1152]{1,0:T(8,128)} %bitcast.12), custom_call_target="tpu_custom_call" | custom-call | tf_op jit(solution)/shard_map/outer_step/pallas_call | solution.py:345
  305.3 0.1 dynamic-slice_bitcast_fusion
  305.4 0.6 collective-permute-start.1
  306.0 1.5 collective-permute-start
  307.5 9.6 %store_outputs.1 = (bf16[2048,4608]{1,0:T(8,128)(2,1)}, f32[2048,1152]{1,0:T(8,128)}) custom-call(bf16[4,2048,1152]{2,1,0:T(8,128)(2,1)S(1)} %get-tuple-element.6.blocks, f32[2048,1152]{1,0:T(8,128)S(1)} %get-tuple-element.7.fresh_moment), custom_call_target="tpu_custom_call" | custom-call | bytes 37748736 | tf_op jit(solution)/shard_map/store_outputs/pallas_call | solution.py:396
  317.1 0.0 collective-permute-done.1.piece_x
  317.1 0.0 collective-permute-done.piece_y
  317.1 1.0 store_tail.1
Async XLA Ops:
  305.4 11.7 %collective-permute-start.1 = (bf16[128,1152]{1,0:T(8,128)(2,1)S(1)}, bf16[128,1152]{1,0:T(8,128)(2,1)S(1)}, u32[]{:S(2)}, u32[]{:S(2)}) collective-permute-start(bf16[128,1152]{1,0:T(8,128)(2,1)S(1)} %get-tuple-element.10), channel_id=1, source_target_pairs={{0,8},{8,0},{16,24},{24,16},{1,9},{9,1},{17,25},{25,17},{2,10},{10... | collective-permute-start | bytes 884744 | tf_op jit(solution)/shard_map/ppermute | solution.py:395
  306.0 11.1 %collective-permute-start = (bf16[128,1152]{1,0:T(8,128)(2,1)S(1)}, bf16[128,1152]{1,0:T(8,128)(2,1)S(1)}, u32[]{:S(2)}, u32[]{:S(2)}) collective-permute-start(bf16[128,1152]{1,0:T(8,128)(2,1)S(1)} %get-tuple-element.11), channel_id=1, source_target_pairs={{0,16},{8,24},{16,0},{24,8},{1,17},{9,25},{17,1},{25,9},{2,18},{10... | collective-permute-start | bytes 884744 | tf_op jit(solution)/shard_map/ppermute | solution.py:394
